TPU v7x, 32 devices: a whole 2x2x4 slice. The times are simulated.
32 devices in a mesh: shards: 4 (over x, core), context: 2 (over y), tensor: 4 (over z).
Axes of the slice: x: 2, y: 2, z: 4, core: 2. Of those that a mesh axis runs over, the one named last changes fastest.
Arguments:
- tokens: bfloat16 [8192, 1280], P(('shards', 'context')), may hold values from -6 to 6
- cotangent: bfloat16 [8192, 1280], P(('shards', 'context')), may hold values from -6 to 6
- segments: int32 [8192], P(('shards', 'context')), may hold values from 0 to 1024, as said below
- positions: int32 [8192], P(('shards', 'context')), may hold values from 0 to 1279, as said below
- w_query: bfloat16 [1280, 1280], P('shards', 'tensor'), may hold values from -0.15625 to 0.15625
- w_key: bfloat16 [1280, 1280], P('shards', 'tensor'), may hold values from -0.15625 to 0.15625
- w_value: bfloat16 [1280, 1280], P('shards', 'tensor'), may hold values from -0.15625 to 0.15625
- w_output: bfloat16 [1280, 1280], P('tensor', 'shards'), may hold values from -0.15625 to 0.15625
- w_up: bfloat16 [1280, 5120], P('shards', 'tensor'), may hold values from -0.15625 to 0.15625
- w_gate: bfloat16 [1280, 5120], P('shards', 'tensor'), may hold values from -0.15625 to 0.15625
- w_down: bfloat16 [5120, 1280], P('tensor', 'shards'), may hold values from -0.078125 to 0.078125
- scale_qk: float32 [1280], P('tensor'), may hold values from 1 to 1.6
- alpha_attn: float32 [1280], replicated, may hold values from 0.15 to 0.6
- alpha_mlp: float32 [1280], replicated, may hold values from 0.15 to 0.6
- scale_up: float32 [5120], P('tensor'), may hold values from 0.25 to 1.75
- scale_gate: float32 [5120], P('tensor'), may hold values from 0.25 to 1.75
Outputs:
- block_out: bfloat16 [8192, 1280], P(('shards', 'context'))
- grad_tokens: bfloat16 [8192, 1280], P(('shards', 'context'))
- grad_query: float32 [1280, 1280], P('shards', 'tensor')
- grad_key: float32 [1280, 1280], P('shards', 'tensor')
- grad_value: float32 [1280, 1280], P('shards', 'tensor')
- grad_output: float32 [1280, 1280], P('tensor', 'shards')
- grad_up: float32 [1280, 5120], P('shards', 'tensor')
- grad_gate: float32 [1280, 5120], P('shards', 'tensor')
- grad_down: float32 [5120, 1280], P('tensor', 'shards')
- grad_scale_qk: float32 [1280], P('tensor')
- grad_alpha_attn: float32 [1280], replicated
- grad_alpha_mlp: float32 [1280], replicated
- grad_scale_up: float32 [5120], P('tensor')
- grad_scale_gate: float32 [5120], P('tensor')
Inputs may be any that keep to these rules, and one draw needn't show every extreme that they name: `segments`: each run of 1024 tokens in order (one device of shards and context) holds first 512 prompt tokens (id 0), the prompt's tokens lying in order over the group, then 512 slots filled with whole continuations of 1 to 256 tokens each, one of exactly 256; a continuation's tokens are consecutive and its id is shared by no other continuation of the group. `positions`: A prompt token's position is its index in the group's prompt; a continuation token's is 1024 plus its offset in its continuation.
All inputs are finite; a program needn't handle non-finite values.
Results may differ from a plain program's by a relative error of at most 0.02.
Values may be sent and summed in bfloat16 or wider, within the bound.
No kernel may reach another device: no remote copies, remote signals or barrier semaphores. Data moves between devices by JAX's collectives and lax.ppermute only.
A program may use at most 192 MiB of HBM per device.

v0:
```python
import math
import jax
import jax.numpy as jnp
from jax import lax
from jax.sharding import PartitionSpec as P

HD = 64
CONT_DEV = 2
CONT_LEN = 256
EPSILON = 1e-06
MASKED = -1e30


def renorm(vector):
    return vector * lax.rsqrt(jnp.mean(vector * vector, axis=-1, keepdims=True) + EPSILON)


def rotate(values, cosine_table, sine_table):
    half_size = values.shape[-1] // 2
    first_half = values[..., :half_size]
    second_half = values[..., half_size:]
    return jnp.concatenate(
        [
            first_half * cosine_table - second_half * sine_table,
            second_half * cosine_table + first_half * sine_table,
        ],
        axis=-1,
    )


def head_norm(raw_heads, cosine_table, sine_table, factor):
    turned = rotate(raw_heads, cosine_table[:, None, :], sine_table[:, None, :])
    return factor * turned * lax.rsqrt(jnp.sum(turned * turned, axis=-1, keepdims=True) + EPSILON)


def residual_step(hidden, branch, alpha):
    return renorm(hidden + alpha * (renorm(branch) - hidden))


def swiglu(up_proj, gate_proj, scale_up, scale_gate):
    return scale_up * up_proj * jax.nn.silu(scale_gate * gate_proj)


def phase_tables(positions, head_size):
    half_size = head_size // 2
    frequency = 10000.0 ** (-(jnp.arange(half_size, dtype=jnp.float32) * 2.0 / head_size))
    phases = positions.astype(jnp.float32)[:, None] * frequency[None, :]
    return (jnp.cos(phases), jnp.sin(phases))


def outer_sum(left, right):
    return lax.dot_general(
        left, right, (((0,), (0,)), ((), ())), preferred_element_type=jnp.float32
    )


def back_product(gradient, weight):
    return lax.dot_general(
        gradient, weight, (((1,), (1,)), ((), ())), preferred_element_type=jnp.float32
    )


def to_heads(flat, head_size):
    return jnp.swapaxes(flat.reshape(flat.shape[0], -1, head_size), 0, 1)


def from_heads(stacked):
    return jnp.swapaxes(stacked, 0, 1).reshape(stacked.shape[1], -1)


def on_device(
    tokens,
    cotangent,
    segments,
    positions,
    w_query,
    w_key,
    w_value,
    w_output,
    w_up,
    w_gate,
    w_down,
    scale_qk,
    alpha_attn,
    alpha_mlp,
    scale_up,
    scale_gate,
):
    full_query, full_key, full_value, full_output, full_up, full_gate, full_down = (
        lax.all_gather(w_query, "shards", axis=0, tiled=True),
        lax.all_gather(w_key, "shards", axis=0, tiled=True),
        lax.all_gather(w_value, "shards", axis=0, tiled=True),
        lax.all_gather(w_output, "shards", axis=1, tiled=True),
        lax.all_gather(w_up, "shards", axis=0, tiled=True),
        lax.all_gather(w_gate, "shards", axis=0, tiled=True),
        lax.all_gather(w_down, "shards", axis=1, tiled=True),
    )
    row_count = tokens.shape[0]
    prompt_rows = row_count - CONT_DEV * CONT_LEN
    heads_local = scale_qk.shape[0] // HD
    multiplier = math.sqrt(HD)
    factor = scale_qk.reshape(heads_local, HD)
    cosine_table, sine_table = phase_tables(positions, HD)

    def normalize(raw_heads, factor_heads):
        return head_norm(raw_heads, cosine_table, sine_table, factor_heads)

    query_raw = jnp.dot(tokens, full_query, preferred_element_type=jnp.float32).reshape(
        row_count, heads_local, HD
    )
    key_raw = jnp.dot(tokens, full_key, preferred_element_type=jnp.float32).reshape(
        row_count, heads_local, HD
    )
    value_low = jnp.dot(tokens, full_value, preferred_element_type=jnp.float32).astype(jnp.bfloat16)
    query_normed, query_back = jax.vjp(normalize, query_raw, factor)
    key_normed, key_back = jax.vjp(normalize, key_raw, factor)
    query_low = query_normed.astype(jnp.bfloat16).reshape(row_count, -1)
    key_low = key_normed.astype(jnp.bfloat16).reshape(row_count, -1)
    prompt_keys, prompt_values = (
        lax.all_gather(key_low[:prompt_rows], "context", axis=0, tiled=True),
        lax.all_gather(value_low[:prompt_rows], "context", axis=0, tiled=True),
    )
    prompt_total = prompt_keys.shape[0]
    key_positions = jnp.concatenate(
        [jnp.arange(prompt_total, dtype=jnp.int32), positions[prompt_rows:]]
    )
    key_segments = jnp.concatenate([jnp.zeros((prompt_total,), jnp.int32), segments[prompt_rows:]])
    allowed = (key_positions[None, :] <= positions[:, None]) & (
        (key_segments[None, :] == 0) | (key_segments[None, :] == segments[:, None])
    )
    key_heads = to_heads(jnp.concatenate([prompt_keys, key_low[prompt_rows:]], axis=0), HD)
    value_heads = to_heads(jnp.concatenate([prompt_values, value_low[prompt_rows:]], axis=0), HD)
    key_heads, value_heads = (key_heads, value_heads)
    query_heads = to_heads(query_low, HD)

    def masked_scores(query_head, key_head):
        scores = multiplier * jnp.einsum(
            "qd,kd->qk", query_head, key_head, preferred_element_type=jnp.float32
        )
        return jnp.where(allowed, scores, MASKED)

    def attend_head(operands):
        query_head, key_head, value_head = operands
        scores = masked_scores(query_head, key_head)
        row_peak = jnp.max(scores, axis=1, keepdims=True)
        weights = jnp.exp(scores - row_peak)
        row_total = jnp.sum(weights, axis=1, keepdims=True)
        softmax_low = (weights / row_total).astype(jnp.bfloat16)
        head_out = jnp.dot(softmax_low, value_head, preferred_element_type=jnp.float32).astype(
            jnp.bfloat16
        )
        return (head_out, (row_peak + jnp.log(row_total))[:, 0])

    mixed_heads, log_totals = lax.map(attend_head, (query_heads, key_heads, value_heads))
    mixed_low = from_heads(mixed_heads)
    attn_terms = jnp.dot(mixed_low, full_output, preferred_element_type=jnp.float32)
    attn_out = lax.psum(attn_terms, "tensor")
    after_attn, attn_back = jax.vjp(residual_step, tokens.astype(jnp.float32), attn_out, alpha_attn)
    after_low = after_attn.astype(jnp.bfloat16)
    up_proj = jnp.dot(after_low, full_up, preferred_element_type=jnp.float32)
    gate_proj = jnp.dot(after_low, full_gate, preferred_element_type=jnp.float32)
    inner, swiglu_back = jax.vjp(swiglu, up_proj, gate_proj, scale_up, scale_gate)
    inner_low = inner.astype(jnp.bfloat16)
    merged_terms = jnp.dot(inner_low, full_down, preferred_element_type=jnp.float32)
    merged = lax.psum(merged_terms, "tensor")
    block_whole, out_back = jax.vjp(residual_step, after_attn, merged, alpha_mlp)
    block_low = block_whole.astype(jnp.bfloat16)
    grad_after, grad_merged, grad_alpha_mlp = out_back(cotangent.astype(jnp.float32))
    merged_grad_low = grad_merged.astype(jnp.bfloat16)
    grad_down = outer_sum(inner_low, merged_grad_low)
    grad_up_proj, grad_gate_proj, grad_scale_up, grad_scale_gate = swiglu_back(
        back_product(merged_grad_low, full_down)
    )
    up_grad_low = grad_up_proj.astype(jnp.bfloat16)
    gate_grad_low = grad_gate_proj.astype(jnp.bfloat16)
    grad_up = outer_sum(after_low, up_grad_low)
    grad_gate = outer_sum(after_low, gate_grad_low)
    input_terms = back_product(up_grad_low, full_up) + back_product(gate_grad_low, full_gate)
    grad_after = grad_after + lax.psum(input_terms, "tensor")
    grad_tokens_direct, grad_attn, grad_alpha_attn = attn_back(grad_after)
    attn_grad_low = grad_attn.astype(jnp.bfloat16)
    grad_output = outer_sum(mixed_low, attn_grad_low)
    grad_mixed_heads = to_heads(back_product(attn_grad_low, full_output).astype(jnp.bfloat16), HD)
    back_keys, back_values = (key_heads, value_heads)

    def head_backward(operands):
        query_head, key_head, value_head, grad_head, log_total = operands
        softmax_full = jnp.exp(masked_scores(query_head, key_head) - log_total[:, None])
        grad_softmax = jnp.einsum(
            "qd,kd->qk", grad_head, value_head, preferred_element_type=jnp.float32
        )
        weighted = jnp.sum(softmax_full * grad_softmax, axis=1, keepdims=True)
        grad_scores = (softmax_full * (grad_softmax - weighted)).astype(jnp.bfloat16)
        grad_query_head = multiplier * jnp.dot(
            grad_scores, key_head, preferred_element_type=jnp.float32
        )
        grad_key_head = multiplier * outer_sum(grad_scores, query_head)
        grad_value_head = outer_sum(softmax_full.astype(jnp.bfloat16), grad_head)
        return (grad_query_head, grad_key_head, grad_value_head)

    grad_query_heads, grad_key_heads, grad_value_heads = lax.map(
        head_backward, (query_heads, back_keys, back_values, grad_mixed_heads, log_totals)
    )
    grad_key_flat = from_heads(grad_key_heads)
    grad_value_flat = from_heads(grad_value_heads)
    prompt_grad_keys, prompt_grad_values = (
        lax.psum_scatter(
            grad_key_flat[:prompt_total].astype(jnp.bfloat16),
            "context",
            scatter_dimension=0,
            tiled=True,
        ).astype(jnp.float32),
        lax.psum_scatter(
            grad_value_flat[:prompt_total].astype(jnp.bfloat16),
            "context",
            scatter_dimension=0,
            tiled=True,
        ).astype(jnp.float32),
    )
    grad_key_rows = jnp.concatenate([prompt_grad_keys, grad_key_flat[prompt_total:]], axis=0)
    grad_value_rows = jnp.concatenate([prompt_grad_values, grad_value_flat[prompt_total:]], axis=0)
    grad_query_raw, grad_factor_query = query_back(
        from_heads(grad_query_heads).reshape(row_count, heads_local, HD)
    )
    grad_key_raw, grad_factor_key = key_back(grad_key_rows.reshape(row_count, heads_local, HD))
    query_grad_low = grad_query_raw.reshape(row_count, -1).astype(jnp.bfloat16)
    key_grad_low = grad_key_raw.reshape(row_count, -1).astype(jnp.bfloat16)
    value_grad_low = grad_value_rows.astype(jnp.bfloat16)
    grad_query = outer_sum(tokens, query_grad_low)
    grad_key = outer_sum(tokens, key_grad_low)
    grad_value = outer_sum(tokens, value_grad_low)
    token_terms = (
        back_product(query_grad_low, full_query)
        + back_product(key_grad_low, full_key)
        + back_product(value_grad_low, full_value)
    )
    grad_tokens = (
        grad_tokens_direct
        + lax.psum(token_terms.astype(jnp.bfloat16), "tensor").astype(jnp.float32)
    ).astype(jnp.bfloat16)
    grad_scale_qk = (grad_factor_query + grad_factor_key).reshape(-1)
    shard_query, shard_key, shard_value, shard_output, shard_up, shard_gate, shard_down = (
        lax.psum_scatter(
            grad_query.astype(jnp.bfloat16), "shards", scatter_dimension=0, tiled=True
        ).astype(jnp.float32),
        lax.psum_scatter(
            grad_key.astype(jnp.bfloat16), "shards", scatter_dimension=0, tiled=True
        ).astype(jnp.float32),
        lax.psum_scatter(
            grad_value.astype(jnp.bfloat16), "shards", scatter_dimension=0, tiled=True
        ).astype(jnp.float32),
        lax.psum_scatter(
            grad_output.astype(jnp.bfloat16), "shards", scatter_dimension=1, tiled=True
        ).astype(jnp.float32),
        lax.psum_scatter(
            grad_up.astype(jnp.bfloat16), "shards", scatter_dimension=0, tiled=True
        ).astype(jnp.float32),
        lax.psum_scatter(
            grad_gate.astype(jnp.bfloat16), "shards", scatter_dimension=0, tiled=True
        ).astype(jnp.float32),
        lax.psum_scatter(
            grad_down.astype(jnp.bfloat16), "shards", scatter_dimension=1, tiled=True
        ).astype(jnp.float32),
    )
    part_query, part_key, part_value, part_output, part_up, part_gate, part_down = (
        lax.psum_scatter(
            shard_query.astype(jnp.bfloat16), "context", scatter_dimension=0, tiled=True
        ).astype(jnp.float32),
        lax.psum_scatter(
            shard_key.astype(jnp.bfloat16), "context", scatter_dimension=0, tiled=True
        ).astype(jnp.float32),
        lax.psum_scatter(
            shard_value.astype(jnp.bfloat16), "context", scatter_dimension=0, tiled=True
        ).astype(jnp.float32),
        lax.psum_scatter(
            shard_output.astype(jnp.bfloat16), "context", scatter_dimension=1, tiled=True
        ).astype(jnp.float32),
        lax.psum_scatter(
            shard_up.astype(jnp.bfloat16), "context", scatter_dimension=0, tiled=True
        ).astype(jnp.float32),
        lax.psum_scatter(
            shard_gate.astype(jnp.bfloat16), "context", scatter_dimension=0, tiled=True
        ).astype(jnp.float32),
        lax.psum_scatter(
            shard_down.astype(jnp.bfloat16), "context", scatter_dimension=1, tiled=True
        ).astype(jnp.float32),
    )
    sum_query, sum_key, sum_value, sum_output, sum_up, sum_gate, sum_down = (
        lax.all_gather(part_query.astype(jnp.bfloat16), "context", axis=0, tiled=True).astype(
            part_query.dtype
        ),
        lax.all_gather(part_key.astype(jnp.bfloat16), "context", axis=0, tiled=True).astype(
            part_key.dtype
        ),
        lax.all_gather(part_value.astype(jnp.bfloat16), "context", axis=0, tiled=True).astype(
            part_value.dtype
        ),
        lax.all_gather(part_output.astype(jnp.bfloat16), "context", axis=1, tiled=True).astype(
            part_output.dtype
        ),
        lax.all_gather(part_up.astype(jnp.bfloat16), "context", axis=0, tiled=True).astype(
            part_up.dtype
        ),
        lax.all_gather(part_gate.astype(jnp.bfloat16), "context", axis=0, tiled=True).astype(
            part_gate.dtype
        ),
        lax.all_gather(part_down.astype(jnp.bfloat16), "context", axis=1, tiled=True).astype(
            part_down.dtype
        ),
    )
    total_scale_qk, total_alpha_attn, total_alpha_mlp, total_scale_up, total_scale_gate = lax.psum(
        (grad_scale_qk, grad_alpha_attn, grad_alpha_mlp, grad_scale_up, grad_scale_gate),
        ("shards", "context"),
    )
    return (
        block_low,
        grad_tokens,
        sum_query,
        sum_key,
        sum_value,
        sum_output,
        sum_up,
        sum_gate,
        sum_down,
        total_scale_qk,
        total_alpha_attn,
        total_alpha_mlp,
        total_scale_up,
        total_scale_gate,
    )


def solution(mesh):
    in_specs = (
        P(("shards", "context"), None),
        P(("shards", "context"), None),
        P(("shards", "context")),
        P(("shards", "context")),
        P("shards", "tensor"),
        P("shards", "tensor"),
        P("shards", "tensor"),
        P("tensor", "shards"),
        P("shards", "tensor"),
        P("shards", "tensor"),
        P("tensor", "shards"),
        P("tensor"),
        P(),
        P(),
        P("tensor"),
        P("tensor"),
    )
    out_specs = (
        P(("shards", "context"), None),
        P(("shards", "context"), None),
        P("shards", "tensor"),
        P("shards", "tensor"),
        P("shards", "tensor"),
        P("tensor", "shards"),
        P("shards", "tensor"),
        P("shards", "tensor"),
        P("tensor", "shards"),
        P("tensor"),
        P(),
        P(),
        P("tensor"),
        P("tensor"),
    )
    return jax.shard_map(
        on_device, mesh=mesh, in_specs=in_specs, out_specs=out_specs, check_vma=False
    )
```

profile of v0, /device:TPU:0, one launch (start us, length us, event | category | flops | bytes accessed | tf_op | source)
XLA Modules:
  0.0 1299.2 jit_solution(2730937836505166477)
XLA Ops:
  11.3 11.3 all_gather.48
  22.7 10.1 all_gather.49
  39.9 10.6 all_gather.50
  55.8 9.5 all_gather.51
  66.5 10.8 all_gather.52
  81.5 57.1 %while.28 = (s32[]{:T(128)}, bf16[5,1024,64]{1,2,0:T(8,128)(2,1)S(1)}, f32[5,1024]{1,0:T(8,128)S(1)}, bf16[5,1024,64]{2,1,0:T(8,128)(2,1)}, bf16[5,1536,64]{2,1,...) while((s32[]{:T(128)}, ...), condition=%wide.region_5.6_spmd.clone, body=%wide.region_2.5_spmd.clone.sunk | while | flops 421592064 | bytes 45289628 | solution.py:154
  100.2 4.2 fusion.137
  111.6 4.2 fusion.137
  140.0 9.3 all_gather.53
  156.1 188.1 %all-reduce.11.cloned.1.call-done = f32[1024,1280]{1,0:T(8,128)} async-done(((f32[1024,1280]{1,0:T(8,128)}), f32[1024,1280]{1,0:T(8,128)}) %all-reduce.11.cloned.1.call-update) | async-done | bytes 5242896 | tf_op jit(solution)/shard_map/psum | solution.py:157
  352.4 8.1 fusion.73
  360.6 8.7 multiply_convert_fusion.4
  369.3 8.7 fusion.74
  378.4 187.5 %all-reduce.13.cloned.1.call-done = f32[1024,1280]{1,0:T(8,128)} async-done(((f32[1024,1280]{1,0:T(8,128)}), f32[1024,1280]{1,0:T(8,128)}) %all-reduce.13.cloned.1.call-update) | async-done | bytes 5242896 | tf_op jit(solution)/shard_map/psum | solution.py:165
  570.0 4.7 fusion.49
  581.1 9.5 multiply_reduce_fusion.1
  595.0 5.5 convolution_add_fusion
  600.8 187.8 %all-reduce.15.cloned.1.call-done = f32[1024,1280]{1,0:T(8,128)} async-done(((f32[1024,1280]{1,0:T(8,128)}), f32[1024,1280]{1,0:T(8,128)}) %all-reduce.15.cloned.1.call-update) | async-done | bytes 5242896 | tf_op jit(solution)/shard_map/psum | solution.py:179
  788.5 9.5 multiply_reduce_fusion.3
  798.1 11.6 multiply_reduce_fusion.4
  814.4 68.5 %while.29 = (s32[]{:T(128)}, f32[5,1024,64]{1,2,0:T(8,128)}, f32[5,1536,64]{1,2,0:T(8,128)}, bf16[5,1536,64]{1,2,0:T(8,128)(2,1)}, bf16[5,1024,64]{2,1,0:T(8,128...) while((s32[]{:T(128)}, f32[5,1024,64]{1,2,0:T(8,128)}, ...), condition=%wide.region_19.20_spmd.clone, body=%wide.region_17.19_spmd.clone.sunk | while | flops 1027243008 | bytes 50515088 | solution.py:201
  816.5 4.5 multiply_reduce_fusion.18
  830.2 4.5 multiply_reduce_fusion.18
  843.9 4.5 multiply_reduce_fusion.18
  857.5 4.5 multiply_reduce_fusion.18
  871.3 4.5 multiply_reduce_fusion.18
  893.8 6.8 convolution_convert_fusion
  902.3 6.7 convolution_convert_fusion.2
  909.2 7.5 convolution_convert_fusion.1
  945.7 40.9 %reduce-scatter.45.cloned.1.call-done = bf16[1280,320]{0,1:T(8,128)(2,1)} async-done(((bf16[1280,1280]{0,1:T(8,128)(2,1)}), bf16[1280,320]{0,1:T(8,128)(2,1)}) %reduce-scatter.45.cloned.1.call-update) | async-done | bytes 819216 | tf_op jit(solution)/shard_map/reduce_scatter | solution.py:261
  986.7 40.9 %reduce-scatter.37.cloned.1.call-done = bf16[320,1280]{1,0:T(8,128)(2,1)} async-done(((bf16[1280,1280]{1,0:T(8,128)(2,1)}), bf16[320,1280]{1,0:T(8,128)(2,1)}) %reduce-scatter.37.cloned.1.call-update) | async-done | bytes 819216 | tf_op jit(solution)/shard_map/reduce_scatter | solution.py:255
  1027.8 40.9 %reduce-scatter.41.cloned.1.call-done = bf16[320,1280]{1,0:T(8,128)(2,1)} async-done(((bf16[1280,1280]{1,0:T(8,128)(2,1)}), bf16[320,1280]{1,0:T(8,128)(2,1)}) %reduce-scatter.41.cloned.1.call-update) | async-done | bytes 819216 | tf_op jit(solution)/shard_map/reduce_scatter | solution.py:258
  1068.8 27.5 %reduce-scatter.57.cloned.1.call-done = bf16[320,320]{1,0:T(8,128)(2,1)} async-done(((bf16[1280,320]{1,0:T(8,128)(2,1)}), bf16[320,320]{1,0:T(8,128)(2,1)}) %reduce-scatter.57.cloned.1.call-update) | async-done | bytes 204816
  1096.3 27.3 %reduce-scatter.53.cloned.1.call-done = bf16[320,320]{1,0:T(8,128)(2,1)} async-done(((bf16[1280,320]{1,0:T(8,128)(2,1)}), bf16[320,320]{1,0:T(8,128)(2,1)}) %reduce-scatter.53.cloned.1.call-update) | async-done | bytes 204816
  1131.5 19.6 %reduce-scatter.49.cloned.1.call-done = bf16[320,320]{1,0:T(8,128)(2,1)} async-done(((bf16[1280,320]{1,0:T(8,128)(2,1)}), bf16[320,320]{1,0:T(8,128)(2,1)}) %reduce-scatter.49.cloned.1.call-update) | async-done | bytes 204816
  1151.3 7.1 add_convert_fusion.1
  1158.5 26.4 %all-reduce.5 = (f32[320]{0:T(512)}, f32[1280]{0:T(1024)}, f32[1280]{0:T(1024)}, f32[1280]{0:T(1024)}, f32[1280]{0:T(1024)}) all-reduce(f32[320]{0:T(512)S(1)} %add.196, f32[1280]{0:T(1024)S(1)} %copy-done.58, f32[1280]{0:T(1024)S(1)} %copy-done.57, ...), channel_id=1, replica_groups=mesh['shards'=4,'context'=2,'tensor'=4] {'shards','context'}, use_global_device_ids=true, to_apply=%region_41.42 | all-reduce | flops 5440 | bytes 43520 | tf_op jit(solution)/shard_map/psum | solution.py:311
  1184.9 5.7 all_gather.60
  1191.6 19.3 %all_gather.63 = bf16[1280,320]{0,1:T(8,128)(2,1)S(1)} all-gather(bf16[1280,160]{0,1:T(8,128)(2,1)} %reduce-scatter.47.cloned.1.call-done), channel_id=1, replica_groups=mesh['shards'=4,'context'=2,'tensor'=4] {'context'}, dimensions={1}, use_global_device_ids=true | all-gather | bytes 1228800 | tf_op jit(solution)/shard_map/all_gather | solution.py:307
  1212.5 13.6 %all_gather.61 = bf16[320,1280]{1,0:T(8,128)(2,1)S(1)} all-gather(bf16[160,1280]{1,0:T(8,128)(2,1)} %reduce-scatter.39.cloned.1.call-done), channel_id=1, replica_groups=mesh['shards'=4,'context'=2,'tensor'=4] {'context'}, dimensions={0}, use_global_device_ids=true | all-gather | bytes 1228800 | tf_op jit(solution)/shard_map/all_gather | solution.py:301
  1227.3 7.2 reduce-scatter.43.cloned.1.call-done
  1234.5 13.6 %all_gather.62 = bf16[320,1280]{1,0:T(8,128)(2,1)S(1)} all-gather(bf16[160,1280]{1,0:T(8,128)(2,1)} %reduce-scatter.43.cloned.1.call-done), channel_id=1, replica_groups=mesh['shards'=4,'context'=2,'tensor'=4] {'context'}, dimensions={0}, use_global_device_ids=true | all-gather | bytes 1228800 | tf_op jit(solution)/shard_map/all_gather | solution.py:304
  1250.1 5.9 all_gather.59
  1256.9 8.7 reduce-scatter.55.cloned.1.call-done
  1265.5 5.7 all_gather.58
  1272.1 7.1 reduce-scatter.51.cloned.1.call-done
  1279.1 5.7 all_gather.57
  1285.7 5.7 add_convert_fusion
  (359 shorter events, 209.4 us)
Async XLA Ops:
  8.0 336.2 %all-reduce.11.cloned.1.call-start = ((), (), s32[]{:S(2)}) async-start(), calls=%async_computation.16 | async-start | bytes 10485760 | tf_op jit(solution)/shard_map/psum | solution.py:157
  22.7 13.3 %copy-start.24 = (bf16[1280,320]{1,0:T(8,128)(2,1)}, bf16[1280,320]{1,0:T(8,128)(2,1)S(1)}, u32[]{:S(2)}) copy-start(bf16[1280,320]{1,0:T(8,128)(2,1)S(1)} %all_gather.48) | copy-start | bytes 2457604
  22.7 13.3 %copy-start.15 = (bf16[1024,1280]{1,0:T(8,128)(2,1)S(1)}, bf16[1024,1280]{1,0:T(8,128)(2,1)}, u32[]{:S(2)}) copy-start(bf16[1024,1280]{1,0:T(8,128)(2,1)} %param.20) | copy-start | bytes 7864324
  38.5 13.1 %copy-start.43 = (f32[1024,5]{0,1:T(8,128)}, f32[1024,5]{0,1:T(8,128)S(1)}, u32[]{:S(2)}) copy-start(f32[1024,5]{0,1:T(8,128)S(1)} %add_rsqrt_fusion) | copy-start | bytes 61444
  39.4 12.1 copy-start.45
  39.5 12.1 copy-start.55
  51.6 13.7 %copy-start.16 = (bf16[1024,1280]{1,0:T(8,128)(2,1)S(1)}, bf16[1024,1280]{1,0:T(8,128)(2,1)}, u32[]{:S(2)}) copy-start(bf16[1024,1280]{1,0:T(8,128)(2,1)} %param.20) | copy-start | bytes 7864324
  66.4 15.1 %copy-start.35 = (bf16[5,1024,64]{1,2,0:T(8,128)(2,1)S(1)}, bf16[5,1024,64]{1,2,0:T(8,128)(2,1)}, u32[]{:S(2)}) copy-start(bf16[5,1024,64]{1,2,0:T(8,128)(2,1)} %custom-call) | copy-start | bytes 1966084
  66.4 15.1 %copy-start.59 = (s32[1024]{0:T(1024)S(1)}, s32[1024]{0:T(1024)}, u32[]{:S(2)}) copy-start(s32[1024]{0:T(1024)} %param.23) | copy-start | bytes 12292
  66.5 15.1 %copy-start.64 = (s32[1024]{0:T(1024)S(1)}, s32[1024]{0:T(1024)}, u32[]{:S(2)}) copy-start(s32[1024]{0:T(1024)} %param.22) | copy-start | bytes 12292
  138.6 15.6 %copy-start.36 = (bf16[5,1024,64]{1,2,0:T(8,128)(2,1)}, bf16[5,1024,64]{1,2,0:T(8,128)(2,1)S(1)}, u32[]{:S(2)}) copy-start(bf16[5,1024,64]{1,2,0:T(8,128)(2,1)S(1)} %get-tuple-element.106) | copy-start | bytes 1966084
  154.3 198.1 %all-gather.6.cloned.1.call-start = ((), (), s32[]{:S(2)}) async-start(), calls=%async_computation.18 | async-start | bytes 4096000 | tf_op jit(solution)/shard_map/all_gather | solution.py:95
  154.9 192.4 %copy-start.53 = (f32[1280]{0:T(1024)S(1)}, f32[1280]{0:T(1024)}, u32[]{:S(2)}) copy-start(f32[1280]{0:T(1024)} %param.32) | copy-start | bytes 15364
  154.9 205.7 %all-gather.4.cloned.1.call-start = ((), (), s32[]{:S(2)}) async-start(), calls=%async_computation.17 | async-start | bytes 4096000 | tf_op jit(solution)/shard_map/all_gather | solution.py:94
  155.5 213.8 %all-gather.8.cloned.1.call-start = ((), (), s32[]{:S(2)}) async-start(), calls=%async_computation.19 | async-start | bytes 4096000 | tf_op jit(solution)/shard_map/all_gather | solution.py:96
  156.0 410.0 %all-reduce.13.cloned.1.call-start = ((), (), s32[]{:S(2)}) async-start(), calls=%async_computation.20 | async-start | bytes 10485760 | tf_op jit(solution)/shard_map/psum | solution.py:165
  352.3 8.2 copy-start.30
  352.4 8.2 copy-start.69
  378.0 191.1 %copy-start.4 = (bf16[1024,1280]{1,0:T(8,128)(2,1)S(1)}, bf16[1024,1280]{1,0:T(8,128)(2,1)}, u32[]{:S(2)}) copy-start(bf16[1024,1280]{1,0:T(8,128)(2,1)} %param.21) | copy-start | bytes 7864324
  378.0 191.1 %copy-start.52 = (f32[1280]{0:T(1024)S(1)}, f32[1280]{0:T(1024)}, u32[]{:S(2)}) copy-start(f32[1280]{0:T(1024)} %param.33) | copy-start | bytes 15364
  378.0 410.5 %all-reduce.15.cloned.1.call-start = ((), (), s32[]{:S(2)}) async-start(), calls=%async_computation.21 | async-start | bytes 10485760 | tf_op jit(solution)/shard_map/psum | solution.py:179
  581.0 9.6 copy-start.32
  581.1 9.6 copy-start.67
  600.5 319.1 %reduce-scatter.33.cloned.1.call-start = ((), (), s32[]{:S(2)}) async-start(), calls=%async_computation.22 | async-start | bytes 983040 | tf_op jit(solution)/shard_map/reduce_scatter | solution.py:207
  788.5 9.5 copy-start.6
  798.0 11.7 slice-start.2
  798.0 11.7 slice-start.3
  885.3 36.2 %reduce-scatter.35.cloned.1.call-start = ((), (), s32[]{:S(2)}) async-start(), calls=%async_computation.23 | async-start | bytes 983040 | tf_op jit(solution)/shard_map/reduce_scatter | solution.py:213
  887.4 58.2 %reduce-scatter.61.cloned.1.call-start = ((), (), s32[]{:S(2)}) async-start(), calls=%async_computation.37 | async-start | bytes 1228800
  893.7 93.0 %reduce-scatter.45.cloned.1.call-start = ((), (), s32[]{:S(2)}) async-start(), calls=%async_computation.29 | async-start | bytes 4096000 | tf_op jit(solution)/shard_map/reduce_scatter | solution.py:261
  900.6 127.1 %reduce-scatter.37.cloned.1.call-start = ((), (), s32[]{:S(2)}) async-start(), calls=%async_computation.25 | async-start | bytes 4096000 | tf_op jit(solution)/shard_map/reduce_scatter | solution.py:255
  909.1 159.6 %reduce-scatter.41.cloned.1.call-start = ((), (), s32[]{:S(2)}) async-start(), calls=%async_computation.27 | async-start | bytes 4096000 | tf_op jit(solution)/shard_map/reduce_scatter | solution.py:258
  916.7 179.5 %reduce-scatter.57.cloned.1.call-start = ((), (), s32[]{:S(2)}) async-start(), calls=%async_computation.35 | async-start | bytes 1228800
  927.8 195.8 %reduce-scatter.53.cloned.1.call-start = ((), (), s32[]{:S(2)}) async-start(), calls=%async_computation.33 | async-start | bytes 1228800
  937.8 213.3 %reduce-scatter.49.cloned.1.call-start = ((), (), s32[]{:S(2)}) async-start(), calls=%async_computation.31 | async-start | bytes 1228800
  942.3 181.5 %copy-start.27 = (bf16[1280,320]{1,0:T(8,128)(2,1)S(1)}, bf16[1280,320]{1,0:T(8,128)(2,1)}, u32[]{:S(2)}) copy-start(bf16[1280,320]{1,0:T(8,128)(2,1)} %copy-done.26) | copy-start | bytes 2457604
  944.6 240.3 %reduce-scatter.63.cloned.1.call-start = ((), (), s32[]{:S(2)}) async-start(), calls=%async_computation.38 | async-start | bytes 368640
  945.7 245.9 %reduce-scatter.47.cloned.1.call-start = ((), (), s32[]{:S(2)}) async-start(), calls=%async_computation.30 | async-start | bytes 1228800 | tf_op jit(solution)/shard_map/reduce_scatter | solution.py:284
  986.7 225.8 %reduce-scatter.39.cloned.1.call-start = ((), (), s32[]{:S(2)}) async-start(), calls=%async_computation.26 | async-start | bytes 1228800 | tf_op jit(solution)/shard_map/reduce_scatter | solution.py:278
  1027.7 206.8 %reduce-scatter.43.cloned.1.call-start = ((), (), s32[]{:S(2)}) async-start(), calls=%async_computation.28 | async-start | bytes 1228800 | tf_op jit(solution)/shard_map/reduce_scatter | solution.py:281
  1068.7 181.4 %reduce-scatter.59.cloned.1.call-start = ((), (), s32[]{:S(2)}) async-start(), calls=%async_computation.36 | async-start | bytes 368640 | tf_op jit(solution)/shard_map/reduce_scatter | solution.py:272
  1096.3 169.3 %reduce-scatter.55.cloned.1.call-start = ((), (), s32[]{:S(2)}) async-start(), calls=%async_computation.34 | async-start | bytes 368640 | tf_op jit(solution)/shard_map/reduce_scatter | solution.py:269
  1123.7 155.5 %reduce-scatter.51.cloned.1.call-start = ((), (), s32[]{:S(2)}) async-start(), calls=%async_computation.32 | async-start | bytes 368640 | tf_op jit(solution)/shard_map/reduce_scatter | solution.py:266
  1127.7 23.6 %copy-start.23 = (bf16[1280,320]{1,0:T(8,128)(2,1)S(1)}, bf16[1280,320]{1,0:T(8,128)(2,1)}, u32[]{:S(2)}) copy-start(bf16[1280,320]{1,0:T(8,128)(2,1)} %copy-done.22) | copy-start | bytes 2457604
  1127.7 23.6 %copy-start.38 = (bf16[512,5,64]{0,2,1:T(8,128)(2,1)S(1)}, bf16[512,5,64]{0,2,1:T(8,128)(2,1)}, u32[]{:S(2)}) copy-start(bf16[512,5,64]{0,2,1:T(8,128)(2,1)} %slice.82) | copy-start | bytes 983044
  1127.7 23.6 %copy-start.47 = (bf16[512,320]{0,1:T(8,128)(2,1)S(1)}, bf16[512,320]{0,1:T(8,128)(2,1)}, u32[]{:S(2)}) copy-start(bf16[512,320]{0,1:T(8,128)(2,1)} %reduce-scatter.35.cloned.1.call-done) | copy-start | bytes 983044
  1151.2 134.5 %all-reduce.17.cloned.1.call-start = ((), (), s32[]{:S(2)}) async-start(), calls=%async_computation.24 | async-start | bytes 5242880 | tf_op jit(solution)/shard_map/psum | solution.py:239
  1227.3 58.4 %copy-start.54 = (f32[1280]{0:T(1024)S(1)}, f32[1280]{0:T(1024)}, u32[]{:S(2)}) copy-start(f32[1280]{0:T(1024)} %param.32) | copy-start | bytes 15364
  (58 other events, 207.2 us)
Sparse Core Ops, SparseCore 0:
  154.4 189.7 all-reduce.10
  378.1 187.8 all-reduce.12
  600.6 187.8 all-reduce.14
  1158.6 104.0 all-reduce.16
Sparse Core Ops, SparseCore 1:
  156.3 29.9 all-gather.5
  187.7 29.1 all-gather.3
  218.3 29.1 all-gather.7
  885.4 14.9 reduce-scatter.32
  902.6 16.0 reduce-scatter.34
  921.3 24.3 reduce-scatter.60
  948.1 38.5 reduce-scatter.44
  989.1 38.5 reduce-scatter.36
  1030.1 38.5 reduce-scatter.40
  1071.9 24.3 reduce-scatter.56
  1099.3 24.3 reduce-scatter.52
  1126.8 24.3 reduce-scatter.48
  1153.3 11.8 reduce-scatter.62
  1167.4 18.7 reduce-scatter.46
  1188.4 24.0 reduce-scatter.38
  1214.7 19.7 reduce-scatter.42
  1236.8 13.3 reduce-scatter.58
  1252.4 13.1 reduce-scatter.54
  1267.6 11.5 reduce-scatter.50
where the time goes:
time: 1310 us; the launch traced here: 1300 us
  waiting for transfers between devices  788 us (60%)
  matrix products  205 us (16%)
  blocking collectives  158 us (12%)
  other arithmetic  74.7 us (6%)
  local copies, waits for them, and re-layouts  54.5 us (4%)
  between operations  17.3 us (1%)
    psum x1, waiting for transfers between devices, on_device(): attn_out = lax.psum(attn_terms, 'tensor')  188 us
    psum x1, waiting for transfers between devices, on_device(): grad_after = grad_after + lax.psum(input_terms, 'tensor')  188 us
    psum x1, waiting for transfers between devices, on_device(): merged = lax.psum(merged_terms, 'tensor')  188 us
    unnamed x28, waiting for transfers between devices  77.3 us
    dot_general x17, matrix products, outer_sum(): lax.dot_general(left, right, (((0,), (0,)), ((), ())), preferred_element_...  51.7 us
    reduce_scatter x1, waiting for transfers between devices, on_device(): lax.psum_scatter(grad_gate.astype(jnp.bfloat16), 'shards', scatter_dimens...  40.9 us
    reduce_scatter x1, waiting for transfers between devices, on_device(): lax.psum_scatter(grad_down.astype(jnp.bfloat16), 'shards', scatter_dimens...  40.9 us
    reduce_scatter x1, waiting for transfers between devices, on_device(): lax.psum_scatter(grad_up.astype(jnp.bfloat16), 'shards', scatter_dimensio...  40.9 us
  transfers between devices with their start and end apart: 23, of which 15 were waited for; matrix products, arithmetic and copies ran while one was open for 8% of the time, Pallas kernels for 0%

commit v1 on v0

--- a/solution.py
+++ b/solution.py
@@ -1,3 +1,4 @@
+import functools
 import math
 import jax
 import jax.numpy as jnp
@@ -9,6 +10,20 @@
 CONT_LEN = 256
 EPSILON = 1e-06
 MASKED = -1e30
+
+
+def write_area(xx, axis_tag):
+    workers = lax.axis_size(axis_tag)
+    taken_in = xx
+    new = lambda z: [(ii, ii ^ z) for ii in range(workers)]
+    for dev in range(workers.bit_length() - 1):
+        parts_out = new(1 << dev)
+        wide_out = lax.ppermute(taken_in, axis_tag, parts_out)
+        taken_in = taken_in + wide_out
+    return taken_in
+
+
+direct_cards = functools.partial(write_area, axis_tag="tensor")
 
 
 def renorm(vector):
@@ -154,7 +169,7 @@
     mixed_heads, log_totals = lax.map(attend_head, (query_heads, key_heads, value_heads))
     mixed_low = from_heads(mixed_heads)
     attn_terms = jnp.dot(mixed_low, full_output, preferred_element_type=jnp.float32)
-    attn_out = lax.psum(attn_terms, "tensor")
+    attn_out = direct_cards(attn_terms)
     after_attn, attn_back = jax.vjp(residual_step, tokens.astype(jnp.float32), attn_out, alpha_attn)
     after_low = after_attn.astype(jnp.bfloat16)
     up_proj = jnp.dot(after_low, full_up, preferred_element_type=jnp.float32)

time: 1310 us -> 1570 us (1.20)
  waiting for transfers between devices: 788 us -> 1040 us
    ppermute x0 -> x2, waiting for transfers between devices: none -> 339 us  [write_area(): wide_out = lax.ppermute(taken_in, axis_tag, parts_out)]
    psum x1 -> x0, waiting for transfers between devices: 188 us -> none  [on_device(): attn_out = lax.psum(attn_terms, 'tensor')]
    psum x1, waiting for transfers between devices: 0.01 us -> 100 us  [on_device(): lax.psum(token_terms.astype(jnp.bfloat16), 'tensor').astype(jnp.float32)]
    unnamed x28 -> x27, waiting for transfers between devices: 77.3 us -> 76.6 us
  transfers between devices with their start and end apart: 23 -> 24, of which waited for: 15 -> 17; matrix products, arithmetic and copies ran while one was open for 8% -> 7% of each run, Pallas kernels for 0% -> 0%
where the time goes in v1:
time: 1570 us; the launch traced here: 1560 us
  waiting for transfers between devices  1040 us (66%)
  matrix products  205 us (13%)
  blocking collectives  156 us (10%)
  other arithmetic  83.4 us (5%)
  local copies, waits for them, and re-layouts  53.4 us (3%)
  between operations  15.9 us (1%)
    ppermute x2, waiting for transfers between devices, write_area(): wide_out = lax.ppermute(taken_in, axis_tag, parts_out)  339 us
    psum x1, waiting for transfers between devices, on_device(): merged = lax.psum(merged_terms, 'tensor')  189 us
    psum x1, waiting for transfers between devices, on_device(): grad_after = grad_after + lax.psum(input_terms, 'tensor')  188 us
    psum x1, waiting for transfers between devices, on_device(): lax.psum(token_terms.astype(jnp.bfloat16), 'tensor').astype(jnp.float32)  100 us
    unnamed x27, waiting for transfers between devices  76.6 us
    dot_general x17, matrix products, outer_sum(): lax.dot_general(left, right, (((0,), (0,)), ((), ())), preferred_element_...  51.7 us
    reduce_scatter x1, waiting for transfers between devices, on_device(): lax.psum_scatter(grad_down.astype(jnp.bfloat16), 'shards', scatter_dimens...  41.2 us
    reduce_scatter x1, waiting for transfers between devices, on_device(): lax.psum_scatter(grad_gate.astype(jnp.bfloat16), 'shards', scatter_dimens...  41.2 us
  transfers between devices with their start and end apart: 24, of which 17 were waited for; matrix products, arithmetic and copies ran while one was open for 7% of the time, Pallas kernels for 0%

profile of v1, /device:TPU:0, one launch (start us, length us, event | category | flops | bytes accessed | tf_op | source)
XLA Modules:
  0.0 1562.1 jit_solution(17469257040741079786)
XLA Ops:
  10.5 11.3 all_gather.48
  21.8 10.1 all_gather.49
  39.1 10.6 all_gather.50
  55.0 9.5 all_gather.51
  65.6 10.8 all_gather.52
  80.7 57.0 %while.28 = (s32[]{:T(128)}, bf16[5,1024,64]{1,2,0:T(8,128)(2,1)S(1)}, f32[5,1024]{1,0:T(8,128)S(1)}, bf16[5,1024,64]{2,1,0:T(8,128)(2,1)}, bf16[5,1536,64]{2,1,...) while((s32[]{:T(128)}, ...), condition=%wide.region_5.6_spmd.clone, body=%wide.region_2.5_spmd.clone.sunk | while | flops 421592064 | bytes 45289628 | solution.py:169
  139.1 9.3 all_gather.53
  154.1 114.0 %collective-permute-done = f32[1024,1280]{1,0:T(8,128)} collective-permute-done((f32[1024,1280]{1,0:T(8,128)}, f32[1024,1280]{1,0:T(8,128)}, u32[]{:S(2)}, u32[]{:S(2)}) %collective-permute-start) | collective-permute-done | bytes 5242912 | tf_op jit(solution)/shard_map/ppermute | solution.py:21
  268.0 7.1 add.187
  278.5 224.6 %collective-permute-done.1 = f32[1024,1280]{1,0:T(8,128)} collective-permute-done((f32[1024,1280]{1,0:T(8,128)}, f32[1024,1280]{1,0:T(8,128)}, u32[]{:S(2)}, u32[]{:S(2)}) %collective-permute-start.1) | collective-permute-done | bytes 5242912 | tf_op jit(solution)/shard_map/ppermute | solution.py:21
  503.1 4.7 multiply_reduce_fusion.11
  512.9 8.1 fusion.73
  521.0 8.7 multiply_convert_fusion.4
  529.7 8.7 fusion.74
  538.9 189.3 %all-reduce.10.cloned.1.call-done = f32[1024,1280]{1,0:T(8,128)} async-done(((f32[1024,1280]{1,0:T(8,128)}), f32[1024,1280]{1,0:T(8,128)}) %all-reduce.10.cloned.1.call-update) | async-done | bytes 5242896 | tf_op jit(solution)/shard_map/psum | solution.py:180
  732.3 4.7 fusion.49
  743.3 9.5 multiply_reduce_fusion.1
  757.2 5.5 convolution_add_fusion
  763.0 187.8 %all-reduce.12.cloned.1.call-done = f32[1024,1280]{1,0:T(8,128)} async-done(((f32[1024,1280]{1,0:T(8,128)}), f32[1024,1280]{1,0:T(8,128)}) %all-reduce.12.cloned.1.call-update) | async-done | bytes 5242896 | tf_op jit(solution)/shard_map/psum | solution.py:194
  950.7 9.5 multiply_reduce_fusion.3
  960.3 11.6 multiply_reduce_fusion.4
  976.7 68.5 %while.29 = (s32[]{:T(128)}, f32[5,1024,64]{1,2,0:T(8,128)}, f32[5,1536,64]{1,2,0:T(8,128)}, bf16[5,1536,64]{1,2,0:T(8,128)(2,1)}, bf16[5,1024,64]{2,1,0:T(8,128...) while((s32[]{:T(128)}, f32[5,1024,64]{1,2,0:T(8,128)}, ...), condition=%wide.region_18.19_spmd.clone, body=%wide.region_16.18_spmd.clone.sunk | while | flops 1027243008 | bytes 50515088 | solution.py:216
  992.4 4.5 multiply_reduce_fusion.18
  1006.1 4.5 multiply_reduce_fusion.18
  1019.8 4.5 multiply_reduce_fusion.18
  1056.1 6.8 convolution_convert_fusion
  1064.6 6.7 convolution_convert_fusion.2
  1071.4 7.5 convolution_convert_fusion.1
  1108.2 41.2 %reduce-scatter.45.cloned.1.call-done = bf16[1280,320]{0,1:T(8,128)(2,1)} async-done(((bf16[1280,1280]{0,1:T(8,128)(2,1)}), bf16[1280,320]{0,1:T(8,128)(2,1)}) %reduce-scatter.45.cloned.1.call-update) | async-done | bytes 819216 | tf_op jit(solution)/shard_map/reduce_scatter | solution.py:276
  1149.5 41.1 %reduce-scatter.37.cloned.1.call-done = bf16[320,1280]{1,0:T(8,128)(2,1)} async-done(((bf16[1280,1280]{1,0:T(8,128)(2,1)}), bf16[320,1280]{1,0:T(8,128)(2,1)}) %reduce-scatter.37.cloned.1.call-update) | async-done | bytes 819216 | tf_op jit(solution)/shard_map/reduce_scatter | solution.py:270
  1190.7 41.2 %reduce-scatter.41.cloned.1.call-done = bf16[320,1280]{1,0:T(8,128)(2,1)} async-done(((bf16[1280,1280]{1,0:T(8,128)(2,1)}), bf16[320,1280]{1,0:T(8,128)(2,1)}) %reduce-scatter.41.cloned.1.call-update) | async-done | bytes 819216 | tf_op jit(solution)/shard_map/reduce_scatter | solution.py:273
  1232.0 27.4 %reduce-scatter.57.cloned.1.call-done = bf16[320,320]{1,0:T(8,128)(2,1)} async-done(((bf16[1280,320]{1,0:T(8,128)(2,1)}), bf16[320,320]{1,0:T(8,128)(2,1)}) %reduce-scatter.57.cloned.1.call-update) | async-done | bytes 204816
  1259.4 27.5 %reduce-scatter.53.cloned.1.call-done = bf16[320,320]{1,0:T(8,128)(2,1)} async-done(((bf16[1280,320]{1,0:T(8,128)(2,1)}), bf16[320,320]{1,0:T(8,128)(2,1)}) %reduce-scatter.53.cloned.1.call-update) | async-done | bytes 204816
  1294.8 19.5 %reduce-scatter.49.cloned.1.call-done = bf16[320,320]{1,0:T(8,128)(2,1)} async-done(((bf16[1280,320]{1,0:T(8,128)(2,1)}), bf16[320,320]{1,0:T(8,128)(2,1)}) %reduce-scatter.49.cloned.1.call-update) | async-done | bytes 204816
  1314.5 7.1 add_convert_fusion.1
  1321.7 26.1 %all-reduce.5 = (f32[320]{0:T(512)}, f32[1280]{0:T(1024)}, f32[1280]{0:T(1024)}, f32[1280]{0:T(1024)}, f32[1280]{0:T(1024)}) all-reduce(f32[320]{0:T(512)S(1)} %add.202, f32[1280]{0:T(1024)S(1)} %copy-done.58, f32[1280]{0:T(1024)S(1)} %copy-done.57, ...), channel_id=1, replica_groups=mesh['shards'=4,'context'=2,'tensor'=4] {'shards','context'}, use_global_device_ids=true, to_apply=%region_40.41 | all-reduce | flops 5440 | bytes 43520 | tf_op jit(solution)/shard_map/psum | solution.py:326
  1347.8 5.7 all_gather.60
  1354.5 18.9 %all_gather.63 = bf16[1280,320]{0,1:T(8,128)(2,1)S(1)} all-gather(bf16[1280,160]{0,1:T(8,128)(2,1)} %reduce-scatter.47.cloned.1.call-done), channel_id=1, replica_groups=mesh['shards'=4,'context'=2,'tensor'=4] {'context'}, dimensions={1}, use_global_device_ids=true | all-gather | bytes 1228800 | tf_op jit(solution)/shard_map/all_gather | solution.py:322
  1375.0 13.0 all_gather.61
  1389.3 7.8 reduce-scatter.43.cloned.1.call-done
  1397.2 12.9 all_gather.62
  1412.9 6.0 all_gather.59
  1419.7 8.5 reduce-scatter.55.cloned.1.call-done
  1428.3 5.7 all_gather.58
  1434.8 7.3 reduce-scatter.51.cloned.1.call-done
  1442.1 5.8 all_gather.57
  1448.7 100.5 %all-reduce.14.cloned.1.call-done = bf16[1024,1280]{1,0:T(8,128)(2,1)} async-done(((bf16[1024,1280]{1,0:T(8,128)(2,1)}), bf16[1024,1280]{1,0:T(8,128)(2,1)}) %all-reduce.14.cloned.1.call-update) | async-done | bytes 2621456 | tf_op jit(solution)/shard_map/psum | solution.py:254
  1549.1 5.7 add_convert_fusion
  (361 shorter events, 227.0 us)
Async XLA Ops:
  7.2 505.7 %all-gather.6.cloned.1.call-start = ((), (), s32[]{:S(2)}) async-start(), calls=%async_computation.17 | async-start | bytes 4096000 | tf_op jit(solution)/shard_map/all_gather | solution.py:110
  21.8 13.3 copy-start.24
  21.8 13.3 copy-start.15
  37.7 13.1 copy-start.43
  38.6 12.1 copy-start.45
  38.7 12.1 copy-start.55
  50.7 13.7 copy-start.16
  65.6 15.1 copy-start.35
  65.6 15.1 copy-start.59
  65.6 15.1 copy-start.64
  137.7 14.7 copy-start.36
  152.4 115.6 %collective-permute-start = (f32[1024,1280]{1,0:T(8,128)}, f32[1024,1280]{1,0:T(8,128)}, u32[]{:S(2)}, u32[]{:S(2)}) collective-permute-start(f32[1024,1280]{1,0:T(8,128)} %fusion.72), channel_id=1, source_target_pairs={{0,1},{1,0},{2,3},{3,2},{4,5},{5,4},{6,7},{7,6},{8,9},{9,8},{10,11... | collective-permute-start | bytes 15728648 | tf_op jit(solution)/shard_map/ppermute | solution.py:21
  154.0 367.0 %all-gather.4.cloned.1.call-start = ((), (), s32[]{:S(2)}) async-start(), calls=%async_computation.16 | async-start | bytes 4096000 | tf_op jit(solution)/shard_map/all_gather | solution.py:109
  275.1 228.0 %collective-permute-start.1 = (f32[1024,1280]{1,0:T(8,128)}, f32[1024,1280]{1,0:T(8,128)}, u32[]{:S(2)}, u32[]{:S(2)}) collective-permute-start(f32[1024,1280]{1,0:T(8,128)} %add.187), channel_id=1, source_target_pairs={{0,2},{1,3},{2,0},{3,1},{4,6},{5,7},{6,4},{7,5},{8,10},{9,11},{10,... | collective-permute-start | bytes 15728648 | tf_op jit(solution)/shard_map/ppermute | solution.py:21
  277.7 252.0 %all-gather.8.cloned.1.call-start = ((), (), s32[]{:S(2)}) async-start(), calls=%async_computation.18 | async-start | bytes 4096000 | tf_op jit(solution)/shard_map/all_gather | solution.py:111
  278.5 229.4 %copy-start.53 = (f32[1280]{0:T(1024)S(1)}, f32[1280]{0:T(1024)}, u32[]{:S(2)}) copy-start(f32[1280]{0:T(1024)} %param.32) | copy-start | bytes 15364
  278.5 449.8 %all-reduce.10.cloned.1.call-start = ((), (), s32[]{:S(2)}) async-start(), calls=%async_computation.19 | async-start | bytes 10485760 | tf_op jit(solution)/shard_map/psum | solution.py:180
  512.8 8.2 copy-start.30
  538.4 192.9 %copy-start.4 = (bf16[1024,1280]{1,0:T(8,128)(2,1)S(1)}, bf16[1024,1280]{1,0:T(8,128)(2,1)}, u32[]{:S(2)}) copy-start(bf16[1024,1280]{1,0:T(8,128)(2,1)} %param.21) | copy-start | bytes 7864324
  538.4 192.9 %copy-start.52 = (f32[1280]{0:T(1024)S(1)}, f32[1280]{0:T(1024)}, u32[]{:S(2)}) copy-start(f32[1280]{0:T(1024)} %param.33) | copy-start | bytes 15364
  538.5 412.3 %all-reduce.12.cloned.1.call-start = ((), (), s32[]{:S(2)}) async-start(), calls=%async_computation.20 | async-start | bytes 10485760 | tf_op jit(solution)/shard_map/psum | solution.py:194
  743.3 9.6 copy-start.32
  743.3 9.6 copy-start.67
  762.7 319.2 %reduce-scatter.33.cloned.1.call-start = ((), (), s32[]{:S(2)}) async-start(), calls=%async_computation.21 | async-start | bytes 983040 | tf_op jit(solution)/shard_map/reduce_scatter | solution.py:222
  950.7 9.5 copy-start.6
  960.3 11.7 slice-start.2
  960.3 11.7 slice-start.3
  1047.6 36.2 %reduce-scatter.35.cloned.1.call-start = ((), (), s32[]{:S(2)}) async-start(), calls=%async_computation.22 | async-start | bytes 983040 | tf_op jit(solution)/shard_map/reduce_scatter | solution.py:228
  1049.7 58.4 %reduce-scatter.61.cloned.1.call-start = ((), (), s32[]{:S(2)}) async-start(), calls=%async_computation.36 | async-start | bytes 1228800
  1056.0 93.4 %reduce-scatter.45.cloned.1.call-start = ((), (), s32[]{:S(2)}) async-start(), calls=%async_computation.28 | async-start | bytes 4096000 | tf_op jit(solution)/shard_map/reduce_scatter | solution.py:276
  1062.9 127.7 %reduce-scatter.37.cloned.1.call-start = ((), (), s32[]{:S(2)}) async-start(), calls=%async_computation.24 | async-start | bytes 4096000 | tf_op jit(solution)/shard_map/reduce_scatter | solution.py:270
  1071.4 160.5 %reduce-scatter.41.cloned.1.call-start = ((), (), s32[]{:S(2)}) async-start(), calls=%async_computation.26 | async-start | bytes 4096000 | tf_op jit(solution)/shard_map/reduce_scatter | solution.py:273
  1079.0 180.3 %reduce-scatter.57.cloned.1.call-start = ((), (), s32[]{:S(2)}) async-start(), calls=%async_computation.34 | async-start | bytes 1228800
  1090.1 196.8 %reduce-scatter.53.cloned.1.call-start = ((), (), s32[]{:S(2)}) async-start(), calls=%async_computation.32 | async-start | bytes 1228800
  1100.1 214.2 %reduce-scatter.49.cloned.1.call-start = ((), (), s32[]{:S(2)}) async-start(), calls=%async_computation.30 | async-start | bytes 1228800
  1104.6 182.4 %copy-start.27 = (bf16[1280,320]{1,0:T(8,128)(2,1)S(1)}, bf16[1280,320]{1,0:T(8,128)(2,1)}, u32[]{:S(2)}) copy-start(bf16[1280,320]{1,0:T(8,128)(2,1)} %copy-done.26) | copy-start | bytes 2457604
  1106.9 240.9 %reduce-scatter.63.cloned.1.call-start = ((), (), s32[]{:S(2)}) async-start(), calls=%async_computation.37 | async-start | bytes 368640
  1108.2 246.3 %reduce-scatter.47.cloned.1.call-start = ((), (), s32[]{:S(2)}) async-start(), calls=%async_computation.29 | async-start | bytes 1228800 | tf_op jit(solution)/shard_map/reduce_scatter | solution.py:299
  1149.5 225.6 %reduce-scatter.39.cloned.1.call-start = ((), (), s32[]{:S(2)}) async-start(), calls=%async_computation.25 | async-start | bytes 1228800 | tf_op jit(solution)/shard_map/reduce_scatter | solution.py:293
  1190.6 206.6 %reduce-scatter.43.cloned.1.call-start = ((), (), s32[]{:S(2)}) async-start(), calls=%async_computation.27 | async-start | bytes 1228800 | tf_op jit(solution)/shard_map/reduce_scatter | solution.py:296
  1231.9 181.0 %reduce-scatter.59.cloned.1.call-start = ((), (), s32[]{:S(2)}) async-start(), calls=%async_computation.35 | async-start | bytes 368640 | tf_op jit(solution)/shard_map/reduce_scatter | solution.py:287
  1259.4 168.9 %reduce-scatter.55.cloned.1.call-start = ((), (), s32[]{:S(2)}) async-start(), calls=%async_computation.33 | async-start | bytes 368640 | tf_op jit(solution)/shard_map/reduce_scatter | solution.py:284
  1287.0 155.1 %reduce-scatter.51.cloned.1.call-start = ((), (), s32[]{:S(2)}) async-start(), calls=%async_computation.31 | async-start | bytes 368640 | tf_op jit(solution)/shard_map/reduce_scatter | solution.py:281
  1291.0 23.5 %copy-start.23 = (bf16[1280,320]{1,0:T(8,128)(2,1)S(1)}, bf16[1280,320]{1,0:T(8,128)(2,1)}, u32[]{:S(2)}) copy-start(bf16[1280,320]{1,0:T(8,128)(2,1)} %copy-done.22) | copy-start | bytes 2457604
  1291.0 23.5 %copy-start.38 = (bf16[512,5,64]{0,2,1:T(8,128)(2,1)S(1)}, bf16[512,5,64]{0,2,1:T(8,128)(2,1)}, u32[]{:S(2)}) copy-start(bf16[512,5,64]{0,2,1:T(8,128)(2,1)} %slice.82) | copy-start | bytes 983044
  1291.0 23.5 %copy-start.47 = (bf16[512,320]{0,1:T(8,128)(2,1)S(1)}, bf16[512,320]{0,1:T(8,128)(2,1)}, u32[]{:S(2)}) copy-start(bf16[512,320]{0,1:T(8,128)(2,1)} %reduce-scatter.35.cloned.1.call-done) | copy-start | bytes 983044
  1314.4 234.7 %all-reduce.14.cloned.1.call-start = ((), (), s32[]{:S(2)}) async-start(), calls=%async_computation.23 | async-start | bytes 5242880 | tf_op jit(solution)/shard_map/psum | solution.py:254
  1389.3 159.8 %copy-start.54 = (f32[1280]{0:T(1024)S(1)}, f32[1280]{0:T(1024)}, u32[]{:S(2)}) copy-start(f32[1280]{0:T(1024)} %param.32) | copy-start | bytes 15364
  (59 other events, 216.4 us)
Sparse Core Ops, SparseCore 0:
  154.1 29.0 all-gather.5
  277.8 28.0 all-gather.3
  307.5 29.2 all-gather.7
  538.6 189.6 all-reduce.9
  762.9 187.8 all-reduce.11
  1047.7 15.0 reduce-scatter.32
  1065.0 16.0 reduce-scatter.34
  1083.7 24.3 reduce-scatter.60
  1110.7 38.6 reduce-scatter.44
  1151.9 38.6 reduce-scatter.36
  1193.2 38.6 reduce-scatter.40
  1234.9 24.3 reduce-scatter.56
  1262.5 24.3 reduce-scatter.52
  1289.9 24.3 reduce-scatter.48
  1316.4 11.9 reduce-scatter.62
  1330.5 18.7 reduce-scatter.46
  1351.4 23.6 reduce-scatter.38
  1377.1 19.9 reduce-scatter.42
  1399.4 13.4 reduce-scatter.58
  1415.0 13.1 reduce-scatter.54
  1430.5 11.5 reduce-scatter.50
  1445.0 104.0 all-reduce.13
